TPU v7x, 512 devices: a whole 4x4x16 slice. The times are simulated.
512 devices in a mesh: virt: 32 (over x, z_lo, core), pair: 16 (over z_hi, y).
Axes of the slice: x: 4, y: 4, z: 16 (z_hi: 4, z_lo: 4; z = z_hi * 4 + z_lo), core: 2. Of those that a mesh axis runs over, the one named last changes fastest.
Arguments:
- amplitudes: float32 [4096, 61440], P('pair', 'virt'), may hold values from -6 to 6
- integrals: float32 [61440, 384], P('virt'), may hold values from -0.09375 to 0.09375
- tile_mask: int32 [640, 4], P('virt'), may hold values from 0 to 1
- mirror_row: int32 [4096], P('pair'), may hold values from 0 to 255, as said below
Outputs:
- residual: float32 [4096, 384], P('pair', 'virt')
Inputs may be any that keep to these rules, and one draw needn't show every extreme that they name: For the row at local index l on pair index q, mirror_row is the local index of its mirror pair's row on pair index (q + G / 2) mod G, G = 16; the rows of one device map one to one onto the rows of that device, and the mirror of the mirror is the row itself.
All inputs are finite; a program needn't handle non-finite values.
Results may differ from a plain program's by a relative error of at most 0.000092.
Values sent between devices are 32-bit elements; how exact they have to be, the bound alone decides.
A program may use at most 64 MiB of HBM per device.

v0:
```python
import jax
import jax.numpy as jnp
from jax import lax
from jax.sharding import PartitionSpec as P

TILE = 96


def shifted(block, axis, distance):
    devices = range(lax.axis_size(axis))
    route = [((i - distance) % len(devices), i) for i in devices]
    return lax.ppermute(block, axis, route)


def product(left_side, right_side):
    return jnp.dot(
        left_side, right_side, precision=lax.Precision.HIGHEST, preferred_element_type=jnp.float32
    )


def shards(amplitudes, integrals, tile_mask, mirror_row):
    tile_rows = integrals.shape[0] // TILE
    col_tiles = integrals.shape[1] // TILE
    grown_view = (
        integrals.reshape(tile_rows, TILE, col_tiles, TILE)
        * tile_mask.astype(jnp.float32)[:, None, :, None]
    )
    masked = grown_view.reshape(integrals.shape)
    pair_size = lax.axis_size("pair")
    virt_size = lax.axis_size("virt")
    partial_value = product(amplitudes, masked)
    reduced = lax.psum_scatter(partial_value, "virt", scatter_dimension=1, tiled=True)
    turned = shifted(reduced, "virt", virt_size // 2)
    turned = shifted(turned, "pair", pair_size // 2)
    return reduced + jnp.take(turned, mirror_row, axis=0)


def solution(mesh):
    in_specs = (P("pair", "virt"), P("virt", None), P("virt", None), P("pair"))
    out_specs = P("pair", "virt")
    return jax.shard_map(shards, mesh=mesh, in_specs=in_specs, out_specs=out_specs, check_vma=False)
```

profile of v0, /device:TPU:160, one launch (start us, length us, event | category | flops | bytes accessed | tf_op | source)
XLA Modules:
  0.0 148.4 jit_solution(13357883231539871842)
XLA Ops:
  0.0 0.8 convert_element_type.3
  0.8 0.1 copy.8
  0.9 2.4 %mul.11 = f32[20,96,4,96]{3,2,1,0:T(4,128)} broadcast(f32[20,4]{1,0:T(8,128)S(1)} %copy.8), dimensions={0,2} | broadcast | bytes 2949440 | tf_op jit(solution)/shard_map/mul | solution.py:25
  3.4 5.3 %mul.12 = f32[1920,384]{1,0:T(8,128)} reshape(f32[20,96,4,96]{3,2,1,0:T(4,128)} %mul.11) | data formatting | bytes 5898240 | tf_op jit(solution)/shard_map/mul | solution.py:25
  8.7 7.5 %fusion.3 = f32[256,384]{0,1:T(8,128)S(1)} fusion(f32[256,1920]{1,0:T(8,128)S(1)} %copy-done, f32[1920,384]{1,0:T(8,128)} %param.5, f32[1920,384]{1,0:T(8,128)} %mul.12), kind=kOutput, calls=%fused_computation.3 | convolution fusion | flops 2265661440 | bytes 8257536 | tf_op jit(solution)/shard_map/dot_general | solution.py:16
  16.2 70.6 %fusion = f32[256,16]{0,1:T(8,128)S(1)} fusion(f32[256,384]{0,1:T(8,128)S(1)} %fusion.3), kind=kCustom, calls=%all-reduce-scatter | all-reduce-scatter fusion | flops 131073 | bytes 411648
  86.8 1.9 %collective-permute-start.2 = (f32[256,16]{0,1:T(8,128)S(1)}, f32[256,16]{0,1:T(8,128)S(1)}, u32[]{:S(2)}, u32[]{:S(2)}) collective-permute-start(f32[256,16]{0,1:T(8,128)S(1)} %fusion), channel_id=1, source_target_pairs={{0,16},{16,32},{32,48},{48,64},{64,80},{80,96},{96,112},{112,128},... | collective-permute-start | bytes 49160
  88.8 1.9 %collective-permute-start.3 = (f32[256,16]{0,1:T(8,128)S(1)}, f32[256,16]{0,1:T(8,128)S(1)}, u32[]{:S(2)}, u32[]{:S(2)}) collective-permute-start(f32[256,16]{0,1:T(8,128)S(1)} %fusion), channel_id=1, source_target_pairs={{0,32},{16,48},{32,64},{48,80},{64,96},{80,112},{96,128},{112,144}... | collective-permute-start | bytes 49160
  90.7 1.3 collective-permute-start.9
  92.0 1.3 collective-permute-start.4
  93.3 2.1 %collective-permute-start.5 = (f32[256,16]{0,1:T(8,128)S(1)}, f32[256,16]{0,1:T(8,128)S(1)}, u32[]{:S(2)}, u32[]{:S(2)}) collective-permute-start(f32[256,16]{0,1:T(8,128)S(1)} %fusion), channel_id=1, source_target_pairs={{0,64},{16,80},{32,96},{48,112},{64,128},{80,144},{96,160},{112,17... | collective-permute-start | bytes 49160
  95.4 5.1 %collective-permute-start.6 = (f32[256,16]{0,1:T(8,128)S(1)}, f32[256,16]{0,1:T(8,128)S(1)}, u32[]{:S(2)}, u32[]{:S(2)}) collective-permute-start(f32[256,16]{0,1:T(8,128)S(1)} %fusion), channel_id=1, source_target_pairs={{0,80},{16,96},{32,112},{48,128},{64,144},{80,160},{96,176},{112,1... | collective-permute-start | bytes 49160
  100.6 9.7 %collective-permute-start.7 = (f32[256,16]{0,1:T(8,128)S(1)}, f32[256,16]{0,1:T(8,128)S(1)}, u32[]{:S(2)}, u32[]{:S(2)}) collective-permute-start(f32[256,16]{0,1:T(8,128)S(1)} %fusion), channel_id=1, source_target_pairs={{0,96},{16,112},{32,128},{48,144},{64,160},{80,176},{96,192},{112,... | collective-permute-start | bytes 49160
  110.2 1.3 collective-permute-start.8
  111.6 1.3 dynamic-slice.4
  113.5 0.9 concatenate
  114.5 0.1 copy.9
  114.6 2.0 %collective-permute-start = (f32[256,12]{1,0:T(8,128)S(1)}, f32[256,12]{1,0:T(8,128)S(1)}, u32[]{:S(2)}, u32[]{:S(2)}) collective-permute-start(f32[256,12]{1,0:T(8,128)S(1)} %copy.9), channel_id=1, source_target_pairs={{256,0},{272,16},{288,32},{304,48},{320,64},{336,80},{352,96},{368... | collective-permute-start | bytes 36872 | tf_op jit(solution)/shard_map/ppermute | solution.py:12
  116.7 6.9 %collective-permute-done = f32[256,12]{1,0:T(8,128)S(1)} collective-permute-done((f32[256,12]{1,0:T(8,128)S(1)}, f32[256,12]{1,0:T(8,128)S(1)}, u32[]{:S(2)}, u32[]{:S(2)}) %collective-permute-start) | collective-permute-done | bytes 12320 | tf_op jit(solution)/shard_map/ppermute | solution.py:12
  123.5 8.4 %collective-permute-start.1 = (f32[256,12]{1,0:T(8,128)S(1)}, f32[256,12]{1,0:T(8,128)S(1)}, u32[]{:S(2)}, u32[]{:S(2)}) collective-permute-start(f32[256,12]{1,0:T(8,128)S(1)} %collective-permute-done), channel_id=1, source_target_pairs={{8,0},{9,1},{10,2},{11,3},{12,4},{13,5},{14,6},{15,7},{0,8},{1,9},... | collective-permute-start | bytes 36872 | tf_op jit(solution)/shard_map/ppermute | solution.py:12
  131.9 15.0 %collective-permute-done.1 = f32[256,12]{1,0:T(8,128)S(1)} collective-permute-done((f32[256,12]{1,0:T(8,128)S(1)}, f32[256,12]{1,0:T(8,128)S(1)}, u32[]{:S(2)}, u32[]{:S(2)}) %collective-permute-start.1) | collective-permute-done | bytes 12320 | tf_op jit(solution)/shard_map/ppermute | solution.py:12
  146.9 0.7 gather_fusion
  147.6 0.1 broadcast_select_fusion
  147.8 0.6 fusion.7
  (18 shorter events, 0.1 us)
Async XLA Ops:
  0.0 8.6 %copy-start = (f32[256,1920]{1,0:T(8,128)S(1)}, f32[256,1920]{1,0:T(8,128)}, u32[]{:S(2)}) copy-start(f32[256,1920]{1,0:T(8,128)} %param.4) | copy-start | bytes 5898244
  8.6 102.9 %copy-start.1 = (s32[256]{0:T(256)S(1)}, s32[256]{0:T(256)}, u32[]{:S(2)}) copy-start(s32[256]{0:T(256)} %param.7) | copy-start | bytes 3076
  86.8 13.7 %collective-permute-start.2 = (f32[256,16]{0,1:T(8,128)S(1)}, f32[256,16]{0,1:T(8,128)S(1)}, u32[]{:S(2)}, u32[]{:S(2)}) collective-permute-start(f32[256,16]{0,1:T(8,128)S(1)} %fusion), channel_id=1, source_target_pairs={{0,16},{16,32},{32,48},{48,64},{64,80},{80,96},{96,112},{112,128},... | collective-permute-start | bytes 49160
  88.8 21.5 %collective-permute-start.3 = (f32[256,16]{0,1:T(8,128)S(1)}, f32[256,16]{0,1:T(8,128)S(1)}, u32[]{:S(2)}, u32[]{:S(2)}) collective-permute-start(f32[256,16]{0,1:T(8,128)S(1)} %fusion), channel_id=1, source_target_pairs={{0,32},{16,48},{32,64},{48,80},{64,96},{80,112},{96,128},{112,144}... | collective-permute-start | bytes 49160
  90.7 4.7 %collective-permute-start.9 = (f32[256,12]{0,1:T(8,128)S(1)}, f32[256,12]{0,1:T(8,128)S(1)}, u32[]{:S(2)}, u32[]{:S(2)}) collective-permute-start(f32[256,12]{0,1:T(8,128)S(1)} %slice.2), channel_id=1, source_target_pairs={{0,128},{16,144},{32,160},{48,176},{64,192},{80,208},{96,224},{112... | collective-permute-start | bytes 36872
  92.0 21.5 %collective-permute-start.4 = (f32[256,16]{0,1:T(8,128)S(1)}, f32[256,16]{0,1:T(8,128)S(1)}, u32[]{:S(2)}, u32[]{:S(2)}) collective-permute-start(f32[256,16]{0,1:T(8,128)S(1)} %fusion), channel_id=1, source_target_pairs={{0,48},{16,64},{32,80},{48,96},{64,112},{80,128},{96,144},{112,160... | collective-permute-start | bytes 49160
  93.3 20.2 %collective-permute-start.5 = (f32[256,16]{0,1:T(8,128)S(1)}, f32[256,16]{0,1:T(8,128)S(1)}, u32[]{:S(2)}, u32[]{:S(2)}) collective-permute-start(f32[256,16]{0,1:T(8,128)S(1)} %fusion), channel_id=1, source_target_pairs={{0,64},{16,80},{32,96},{48,112},{64,128},{80,144},{96,160},{112,17... | collective-permute-start | bytes 49160
  95.4 18.1 %collective-permute-start.6 = (f32[256,16]{0,1:T(8,128)S(1)}, f32[256,16]{0,1:T(8,128)S(1)}, u32[]{:S(2)}, u32[]{:S(2)}) collective-permute-start(f32[256,16]{0,1:T(8,128)S(1)} %fusion), channel_id=1, source_target_pairs={{0,80},{16,96},{32,112},{48,128},{64,144},{80,160},{96,176},{112,1... | collective-permute-start | bytes 49160
  100.6 13.0 %collective-permute-start.7 = (f32[256,16]{0,1:T(8,128)S(1)}, f32[256,16]{0,1:T(8,128)S(1)}, u32[]{:S(2)}, u32[]{:S(2)}) collective-permute-start(f32[256,16]{0,1:T(8,128)S(1)} %fusion), channel_id=1, source_target_pairs={{0,96},{16,112},{32,128},{48,144},{64,160},{80,176},{96,192},{112,... | collective-permute-start | bytes 49160
  110.2 3.3 %collective-permute-start.8 = (f32[256,16]{0,1:T(8,128)S(1)}, f32[256,16]{0,1:T(8,128)S(1)}, u32[]{:S(2)}, u32[]{:S(2)}) collective-permute-start(f32[256,16]{0,1:T(8,128)S(1)} %fusion), channel_id=1, source_target_pairs={{0,112},{16,128},{32,144},{48,160},{64,176},{80,192},{96,208},{112... | collective-permute-start | bytes 49160
  114.6 8.9 %collective-permute-start = (f32[256,12]{1,0:T(8,128)S(1)}, f32[256,12]{1,0:T(8,128)S(1)}, u32[]{:S(2)}, u32[]{:S(2)}) collective-permute-start(f32[256,12]{1,0:T(8,128)S(1)} %copy.9), channel_id=1, source_target_pairs={{256,0},{272,16},{288,32},{304,48},{320,64},{336,80},{352,96},{368... | collective-permute-start | bytes 36872 | tf_op jit(solution)/shard_map/ppermute | solution.py:12
  123.5 23.3 %collective-permute-start.1 = (f32[256,12]{1,0:T(8,128)S(1)}, f32[256,12]{1,0:T(8,128)S(1)}, u32[]{:S(2)}, u32[]{:S(2)}) collective-permute-start(f32[256,12]{1,0:T(8,128)S(1)} %collective-permute-done), channel_id=1, source_target_pairs={{8,0},{9,1},{10,2},{11,3},{12,4},{13,5},{14,6},{15,7},{0,8},{1,9},... | collective-permute-start | bytes 36872 | tf_op jit(solution)/shard_map/ppermute | solution.py:12
where the time goes:
time: 149 us; the launch traced here: 148 us
  blocking collectives  70.6 us (47%)
  starting transfers between devices  35 us (23%)
  waiting for transfers between devices  21.8 us (15%)
  local copies, waits for them, and re-layouts  11 us (7%)
  matrix products  7.54 us (5%)
  other arithmetic  1.57 us (1%)
    unnamed x1, blocking collectives  70.6 us
    unnamed x8, starting transfers between devices  24.6 us
    ppermute x2, waiting for transfers between devices, shifted(): return lax.ppermute(block, axis, route)  21.8 us
    ppermute x2, starting transfers between devices, shifted(): return lax.ppermute(block, axis, route)  10.4 us
    mul x2, local copies, waits for them, and re-layouts, shards(): integrals.reshape(tile_rows, TILE, col_tiles, TILE)  7.72 us
    dot_general x1, matrix products, product(): jnp.dot(left_side, right_side, precision=lax.Precision.HIGHEST, preferred...  7.54 us
  transfers between devices with their start and end apart: 10, of which 2 were waited for; matrix products, arithmetic and copies ran while one was open for 1% of the time, Pallas kernels for 0%

commit v1 on v0

v1 whole, which is shorter than its diff:
```python
import functools

import jax
import jax.numpy as jnp
from jax import lax
from jax.experimental import pallas as pl
from jax.experimental.pallas import tpu as pltpu
from jax.sharding import PartitionSpec as P

TILE = 96
CHUNKS = ((0, 768), (768, 768), (1536, 384))
F32 = jnp.float32
BF16 = jnp.bfloat16


def split(value):
    high = value.astype(BF16)
    return high, (value - high.astype(F32)).astype(BF16)


def dot(left, right):
    return jnp.dot(left, right, preferred_element_type=F32)


def remote(src, dst, send, recv, virt, pair):
    return pltpu.make_async_remote_copy(
        src_ref=src,
        dst_ref=dst,
        send_sem=send,
        recv_sem=recv,
        device_id={"virt": virt, "pair": pair},
        device_id_type=pl.DeviceIdType.MESH,
    )


def kernel(
    amp_hbm,
    int_hbm,
    mask_ref,
    mirror_ref,
    out_ref,
    amp,
    ints,
    part,
    part_in,
    summed,
    x_in,
    x_sum,
    z_in,
    final,
    own_in,
    mirror_in,
    select,
    load_sem,
    send_sem,
    recv_sem,
):
    virt = lax.axis_index("virt")
    pair = lax.axis_index("pair")
    core = virt % 2
    z = (virt // 2) % 4
    x = virt // 8
    other = 1 - core

    def at(xx, zz, cc):
        return xx * 8 + zz * 2 + cc

    partner = at(x, z, other)
    x_peers = [at((x + d) % 4, z, core) for d in (1, 2, 3)]
    z_peers = [at(x, (z + d) % 4, core) for d in (1, 2, 3)]
    far_pair = (pair + 8) % 16
    far = [at((x + 2) % 4, z, cc) for cc in (0, 1)]

    barrier = pltpu.get_barrier_semaphore()
    for peer in [*x_peers, *z_peers, partner]:
        pl.semaphore_signal(
            barrier, inc=1, device_id={"virt": peer, "pair": pair}, device_id_type=pl.DeviceIdType.MESH
        )
    for peer in far:
        pl.semaphore_signal(
            barrier, inc=1, device_id={"virt": peer, "pair": far_pair}, device_id_type=pl.DeviceIdType.MESH
        )

    loads = []
    for i, (start, size) in enumerate(CHUNKS):
        for j, (src, dst) in enumerate(
            (
                (int_hbm.at[pl.ds(start, size), :], ints.at[pl.ds(start, size), :]),
                (amp_hbm.at[:, pl.ds(start, size)], amp.at[:, pl.ds(start, size)]),
            )
        ):
            copy = pltpu.make_async_copy(src, dst, load_sem.at[2 * i + j])
            copy.start()
            loads.append(copy)

    lane_tile = lax.broadcasted_iota(jnp.int32, (4, 384), 1) // TILE
    row_tile = lax.broadcasted_iota(jnp.int32, (4, 384), 0)
    spread = (lane_tile == row_tile).astype(F32)
    mask = lax.dot_general(
        mask_ref[...].astype(F32), spread, (((0,), (0,)), ((), ())), preferred_element_type=F32
    )
    rows = lax.broadcasted_iota(jnp.int32, (256, 256), 0)
    select[...] = (rows == mirror_ref[...]).astype(F32).astype(BF16)

    total = jnp.zeros((256, 384), F32)
    for i, (start, size) in enumerate(CHUNKS):
        loads[2 * i].wait()
        loads[2 * i + 1].wait()
        tiles = []
        for t in range(start // TILE, (start + size) // TILE):
            tiles.append(ints[t * TILE : (t + 1) * TILE, :] * mask[t : t + 1, :])
        b_high, b_low = split(jnp.concatenate(tiles, axis=0))
        a_high, a_low = split(amp[:, start : start + size])
        total += dot(a_high, b_high) + dot(a_high, b_low) + dot(a_low, b_high)
    part[0] = total[:128].T
    part[1] = total[128:].T

    pl.semaphore_wait(barrier, 9)

    sends = []

    def send(slot, src, dst, virt_to, pair_to):
        copy = remote(src, dst, send_sem.at[slot], recv_sem.at[slot], virt_to, pair_to)
        copy.start()
        sends.append(copy)

    send(0, part.at[other], part_in, partner, pair)
    sends[0].wait_recv()
    summed[...] = part[core] + part_in[...]

    for d in (1, 2, 3):
        block = pl.ds(((x + d) % 4) * 96, 96)
        send(d, summed.at[block], x_in.at[d - 1], x_peers[d - 1], pair)
    for d in (1, 2, 3):
        sends[d].wait_recv()
    x_sum[...] = summed[pl.ds(x * 96, 96), :] + x_in[0] + x_in[1] + x_in[2]

    for d in (1, 2, 3):
        block = pl.ds(((z + d) % 4) * 24, 24)
        send(3 + d, x_sum.at[block], z_in.at[d - 1], z_peers[d - 1], pair)
    for d in (1, 2, 3):
        sends[3 + d].wait_recv()
    final[...] = x_sum[pl.ds(z * 24, 24), :] + z_in[0] + z_in[1] + z_in[2]

    for cc in (0, 1):
        copy = remote(
            final.at[pl.ds(8 * cc, 16)],
            mirror_in.at[core],
            send_sem.at[7 + cc],
            recv_sem.at[7 + core],
            far[cc],
            far_pair,
        )
        copy.start()
        sends.append(copy)
    send(9, final.at[pl.ds(8 * other, 16)], own_in, partner, pair)

    def pick(value):
        return jnp.where(core == 0, value[0:12], value[4:16])

    sends[9].wait_recv()
    mine = final[...]
    mine = jnp.where(core == 0, mine[0:12], mine[12:24])
    theirs = pick(own_in[...])
    low_half = jnp.where(core == 0, mine, theirs)
    high_half = jnp.where(core == 0, theirs, mine)
    own = jnp.concatenate([low_half, high_half], axis=1)

    for half in (0, 1):
        pltpu.make_async_copy(mirror_in.at[half], mirror_in.at[half], recv_sem.at[7 + half]).wait()
    turned = jnp.concatenate([pick(mirror_in[0]), pick(mirror_in[1])], axis=1)
    first, rest = turned.astype(BF16), turned
    rest = turned - first.astype(F32)
    second = rest.astype(BF16)
    third = (rest - second.astype(F32)).astype(BF16)
    matrix = select[...]
    out_ref[...] = own + (dot(first, matrix) + dot(second, matrix) + dot(third, matrix))

    for copy in sends:
        copy.wait_send()


def shards(amplitudes, integrals, tile_mask, mirror_row):
    any_spec = pl.BlockSpec(memory_space=pl.ANY)
    vmem_spec = pl.BlockSpec(memory_space=pltpu.VMEM)
    result = pl.pallas_call(
        kernel,
        out_shape=jax.ShapeDtypeStruct((12, 256), F32),
        in_specs=[any_spec, any_spec, vmem_spec, vmem_spec],
        out_specs=vmem_spec,
        scratch_shapes=[
            pltpu.VMEM((256, 1920), F32),
            pltpu.VMEM((1920, 384), F32),
            pltpu.VMEM((2, 384, 128), F32),
            pltpu.VMEM((384, 128), F32),
            pltpu.VMEM((384, 128), F32),
            pltpu.VMEM((3, 96, 128), F32),
            pltpu.VMEM((96, 128), F32),
            pltpu.VMEM((3, 24, 128), F32),
            pltpu.VMEM((24, 128), F32),
            pltpu.VMEM((16, 128), F32),
            pltpu.VMEM((2, 16, 128), F32),
            pltpu.VMEM((256, 256), BF16),
            pltpu.SemaphoreType.DMA((6,)),
            pltpu.SemaphoreType.DMA((10,)),
            pltpu.SemaphoreType.DMA((10,)),
        ],
        compiler_params=pltpu.CompilerParams(collective_id=0, has_side_effects=True),
        name="ladder",
    )(amplitudes, integrals, tile_mask.T, mirror_row.reshape(1, 256))
    return result.T


def solution(mesh):
    in_specs = (P("pair", "virt"), P("virt", None), P("virt", None), P("pair"))
    out_specs = P("pair", "virt")
    return jax.shard_map(shards, mesh=mesh, in_specs=in_specs, out_specs=out_specs, check_vma=False)
```

time: 149 us -> 36 us (0.24)
  the two profiles are of different devices: /device:TPU:160 before, /device:TPU:1 now
where the time goes in v1:
time: 36 us; the launch traced here: 35.8 us
  Pallas kernels  34.5 us (96%)
  local copies, waits for them, and re-layouts  1.32 us (4%)
    pallas_call x1, Pallas kernels, shards(): pl.pallas_call(kernel, out_shape=jax.ShapeDtypeStruct((12, 256), F32), in...  34.5 us
    unnamed x1, local copies, waits for them, and re-layouts  1.32 us

profile of v1, /device:TPU:1, one launch (start us, length us, event | category | flops | bytes accessed | tf_op | source)
XLA Modules:
  0.0 35.8 jit_solution(15435513148670293464)
XLA Ops:
  0.0 34.5 %ladder.1 = f32[12,256]{1,0:T(8,128)} custom-call(f32[256,1920]{1,0:T(8,128)} %amp_hbm.1, f32[1920,384]{1,0:T(8,128)} %int_hbm.1, s32[4,20]{1,0:T(4,128)} %bitcast.4, s32[1,256]{1,0:T(1,128)} %bitcast.5), custom_call_target="tpu_custom_call" | custom-call | tf_op jit(solution)/shard_map/ladder/pallas_call | solution.py:186
  34.5 1.3 %copy.6 = f32[256,12]{0,1:T(8,128)} copy(f32[256,12]{0,1:T(8,128)} %bitcast.3) | data formatting | bytes 24576

commit v2 on v0

v2 whole, which is shorter than its diff:
```python
import jax
import jax.numpy as jnp
from jax import lax
from jax.experimental import pallas as pl
from jax.experimental.pallas import tpu as pltpu
from jax.sharding import PartitionSpec as P

TILE = 96
CHUNKS = ((0, 768), (768, 768), (1536, 384))
F32 = jnp.float32
BF16 = jnp.bfloat16
MESH = pl.DeviceIdType.MESH


def split(value):
    high = value.astype(BF16)
    return high, (value - high.astype(F32)).astype(BF16)


def dot(left, right):
    return jnp.dot(left, right, preferred_element_type=F32)


def unpack(block):
    return jnp.concatenate([block[0:12], block[12:24]], axis=1)


def kernel(
    amp_hbm,
    int_hbm,
    mask_hbm,
    mirror_hbm,
    out_ref,
    amp,
    ints,
    mask_in,
    mirror_row,
    part,
    part_in,
    summed,
    far_x_in,
    far_x_sum,
    far_in,
    own_x_in,
    own_x_sum,
    own_z_in,
    select,
    load_sem,
    send_sem,
    recv_sem,
):
    loads = [pltpu.make_async_copy(mask_hbm, mask_in, load_sem.at[0])]
    for i, (start, size) in enumerate(CHUNKS):
        loads.append(
            pltpu.make_async_copy(
                int_hbm.at[pl.ds(start, size), :], ints.at[pl.ds(start, size), :], load_sem.at[2 * i + 1]
            )
        )
        loads.append(
            pltpu.make_async_copy(
                amp_hbm.at[:, pl.ds(start, size)], amp.at[:, pl.ds(start, size)], load_sem.at[2 * i + 2]
            )
        )
    loads.append(pltpu.make_async_copy(mirror_hbm, mirror_row, load_sem.at[7]))
    for load in loads:
        load.start()

    virt = lax.axis_index("virt")
    pair = lax.axis_index("pair")
    core = virt % 2
    z = (virt // 2) % 4
    x = virt // 8
    other = 1 - core
    far_pair = (pair + 8) % 16

    def at(xx, zz, cc):
        return xx * 8 + zz * 2 + cc

    partner = at(x, z, other)
    x_peers = [at((x + d) % 4, z, core) for d in (1, 2, 3)]
    z_peers = [at(x, (z + d) % 4, core) for d in (1, 2, 3)]
    far_peers = [at(x, (z + d) % 4, core) for d in (0, 1, 2, 3)]

    barrier = pltpu.get_barrier_semaphore()
    for peer in far_peers:
        pl.semaphore_signal(barrier, inc=1, device_id={"virt": peer, "pair": far_pair}, device_id_type=MESH)
    for peer in [*x_peers, *z_peers, partner]:
        pl.semaphore_signal(barrier, inc=1, device_id={"virt": peer, "pair": pair}, device_id_type=MESH)

    lane_tile = lax.broadcasted_iota(jnp.int32, (4, 384), 1) // TILE
    row_tile = lax.broadcasted_iota(jnp.int32, (4, 384), 0)
    spread = (lane_tile == row_tile).astype(F32)
    loads[0].wait()
    mask = lax.dot_general(
        mask_in[...].astype(F32), spread, (((0,), (0,)), ((), ())), preferred_element_type=F32
    )

    total = jnp.zeros((256, 384), F32)
    for i, (start, size) in enumerate(CHUNKS):
        loads[2 * i + 1].wait()
        loads[2 * i + 2].wait()
        tiles = []
        for t in range(start // TILE, (start + size) // TILE):
            tiles.append(ints[t * TILE : (t + 1) * TILE, :] * mask[t : t + 1, :])
        b_high, b_low = split(jnp.concatenate(tiles, axis=0))
        a_high, a_low = split(amp[:, start : start + size])
        total += dot(a_high, b_high) + dot(a_high, b_low) + dot(a_low, b_high)
    left = total[:128].T
    right = total[128:].T
    for cc in (0, 1):
        for b in range(16):
            first = 24 * b + 12 * cc
            part[cc, b] = jnp.concatenate([left[first : first + 12], right[first : first + 12]], axis=0)

    pl.semaphore_wait(barrier, 11)

    sends = []

    def send(slot, src, dst, virt_to, pair_to):
        copy = pltpu.make_async_remote_copy(
            src_ref=src,
            dst_ref=dst,
            send_sem=send_sem.at[slot],
            recv_sem=recv_sem.at[slot],
            device_id={"virt": virt_to, "pair": pair_to},
            device_id_type=MESH,
        )
        copy.start()
        sends.append(copy)
        return copy

    order = (2, 1, 3, 0)
    halves = []
    for i, d in enumerate(order):
        block = pl.ds(((x + 2 + d) % 4) * 4, 4)
        halves.append(send(i, part.at[other, block], part_in.at[i], partner, pair))

    loads[7].wait()
    rows = lax.broadcasted_iota(jnp.int32, (256, 256), 0)
    select[...] = (rows == mirror_row[...]).astype(F32).astype(BF16)

    arrivals = []
    for i, d in enumerate(order):
        block = pl.ds(((x + 2 + d) % 4) * 4, 4)
        halves[i].wait_recv()
        summed[block] = part[core, block] + part_in[i]
        if d:
            arrivals.append(send(3 + d, summed.at[block], far_x_in.at[d - 1], x_peers[d - 1], pair))
    for copy in arrivals:
        copy.wait_recv()
    far_x_sum[...] = summed[pl.ds(((x + 2) % 4) * 4, 4)] + far_x_in[0] + far_x_in[1] + far_x_in[2]

    far = []
    for d in (0, 1, 3, 2):
        copy = pltpu.make_async_remote_copy(
            src_ref=far_x_sum.at[(z + d) % 4],
            dst_ref=far_in.at[d],
            send_sem=send_sem.at[7 + d],
            recv_sem=recv_sem.at[7 + d],
            device_id={"virt": far_peers[d], "pair": far_pair},
            device_id_type=MESH,
        )
        copy.start()
        sends.append(copy)
        far.append(copy)

    arrivals = []
    for d in (2, 1, 3):
        block = pl.ds(((x + d) % 4) * 4, 4)
        arrivals.append(send(10 + d, summed.at[block], own_x_in.at[d - 1], x_peers[d - 1], pair))
    for copy in arrivals:
        copy.wait_recv()
    own_x_sum[...] = summed[pl.ds(x * 4, 4)] + own_x_in[0] + own_x_in[1] + own_x_in[2]
    arrivals = []
    for d in (1, 2, 3):
        arrivals.append(send(13 + d, own_x_sum.at[(z + d) % 4], own_z_in.at[d - 1], z_peers[d - 1], pair))
    for copy in arrivals:
        copy.wait_recv()
    own = unpack(own_x_sum[z] + own_z_in[0] + own_z_in[1] + own_z_in[2])

    for copy in far:
        copy.wait_recv()
    turned = unpack(far_in[0] + far_in[1] + far_in[2] + far_in[3])
    first = turned.astype(BF16)
    rest = turned - first.astype(F32)
    second, third = split(rest)
    matrix = select[...]
    out_ref[...] = own + (dot(first, matrix) + dot(second, matrix) + dot(third, matrix))

    for copy in sends:
        copy.wait_send()


def shards(amplitudes, integrals, tile_mask, mirror_row):
    any_spec = pl.BlockSpec(memory_space=pl.ANY)
    result = pl.pallas_call(
        kernel,
        out_shape=jax.ShapeDtypeStruct((12, 256), F32),
        in_specs=[any_spec] * 4,
        out_specs=pl.BlockSpec(memory_space=pltpu.VMEM),
        scratch_shapes=[
            pltpu.VMEM((256, 1920), F32),
            pltpu.VMEM((1920, 384), F32),
            pltpu.VMEM((4, 20), jnp.int32),
            pltpu.VMEM((1, 256), jnp.int32),
            pltpu.VMEM((2, 16, 24, 128), F32),
            pltpu.VMEM((4, 4, 24, 128), F32),
            pltpu.VMEM((16, 24, 128), F32),
            pltpu.VMEM((3, 4, 24, 128), F32),
            pltpu.VMEM((4, 24, 128), F32),
            pltpu.VMEM((4, 24, 128), F32),
            pltpu.VMEM((3, 4, 24, 128), F32),
            pltpu.VMEM((4, 24, 128), F32),
            pltpu.VMEM((3, 24, 128), F32),
            pltpu.VMEM((256, 256), BF16),
            pltpu.SemaphoreType.DMA((8,)),
            pltpu.SemaphoreType.DMA((17,)),
            pltpu.SemaphoreType.DMA((17,)),
        ],
        compiler_params=pltpu.CompilerParams(collective_id=0, has_side_effects=True),
        name="ladder",
    )(amplitudes, integrals, tile_mask.T, mirror_row.reshape(1, 256))
    return result.T


def solution(mesh):
    in_specs = (P("pair", "virt"), P("virt", None), P("virt", None), P("pair"))
    out_specs = P("pair", "virt")
    return jax.shard_map(shards, mesh=mesh, in_specs=in_specs, out_specs=out_specs, check_vma=False)
```

time: 149 us -> 31.4 us (0.21)
  the two profiles are of different devices: /device:TPU:160 before, /device:TPU:24 now
where the time goes in v2:
time: 31.4 us; the launch traced here: 31.2 us
  Pallas kernels  29.9 us (95%)
  local copies, waits for them, and re-layouts  1.32 us (4%)
    pallas_call x1, Pallas kernels, shards(): pl.pallas_call(kernel, out_shape=jax.ShapeDtypeStruct((12, 256), F32), in...  29.9 us
    unnamed x1, local copies, waits for them, and re-layouts  1.32 us

profile of v2, /device:TPU:24, one launch (start us, length us, event | category | flops | bytes accessed | tf_op | source)
XLA Modules:
  0.0 31.2 jit_solution(9487125625113717355)
XLA Ops:
  0.0 29.9 %ladder.1 = f32[12,256]{1,0:T(8,128)} custom-call(f32[256,1920]{1,0:T(8,128)} %amp_hbm.1, f32[1920,384]{1,0:T(8,128)} %int_hbm.1, s32[4,20]{1,0:T(4,128)} %bitcast.4, s32[1,256]{1,0:T(1,128)} %bitcast.5), custom_call_target="tpu_custom_call" | custom-call | tf_op jit(solution)/shard_map/ladder/pallas_call | solution.py:196
  29.9 1.3 %copy.6 = f32[256,12]{0,1:T(8,128)} copy(f32[256,12]{0,1:T(8,128)} %bitcast.3) | data formatting | bytes 24576

commit v3 on v2

--- a/solution.py
+++ b/solution.py
@@ -48,6 +48,8 @@
     load_sem,
     send_sem,
     recv_sem,
+    next_sem,
+    far_sem,
 ):
     loads = [pltpu.make_async_copy(mask_hbm, mask_in, load_sem.at[0])]
     for i, (start, size) in enumerate(CHUNKS):
@@ -82,10 +84,16 @@
     far_peers = [at(x, (z + d) % 4, core) for d in (0, 1, 2, 3)]
 
     barrier = pltpu.get_barrier_semaphore()
-    for peer in far_peers:
-        pl.semaphore_signal(barrier, inc=1, device_id={"virt": peer, "pair": far_pair}, device_id_type=MESH)
-    for peer in [*x_peers, *z_peers, partner]:
-        pl.semaphore_signal(barrier, inc=1, device_id={"virt": peer, "pair": pair}, device_id_type=MESH)
+
+    def signal(semaphore, virt_to, pair_to):
+        pl.semaphore_signal(semaphore, inc=1, device_id={"virt": virt_to, "pair": pair_to}, device_id_type=MESH)
+
+    next_pair = (pair + 4) % 16
+    last_pair = (pair + 12) % 16
+    signal(barrier, virt, next_pair)
+    signal(barrier, virt, last_pair)
+    for peer in [*z_peers, *x_peers, partner]:
+        signal(barrier, peer, pair)
 
     lane_tile = lax.broadcasted_iota(jnp.int32, (4, 384), 1) // TILE
     row_tile = lax.broadcasted_iota(jnp.int32, (4, 384), 0)
@@ -99,6 +107,9 @@
     for i, (start, size) in enumerate(CHUNKS):
         loads[2 * i + 1].wait()
         loads[2 * i + 2].wait()
+        if i == len(CHUNKS) - 1:
+            pl.semaphore_wait(barrier, 9)
+            signal(next_sem, virt, last_pair)
         tiles = []
         for t in range(start // TILE, (start + size) // TILE):
             tiles.append(ints[t * TILE : (t + 1) * TILE, :] * mask[t : t + 1, :])
@@ -107,12 +118,13 @@
         total += dot(a_high, b_high) + dot(a_high, b_low) + dot(a_low, b_high)
     left = total[:128].T
     right = total[128:].T
-    for cc in (0, 1):
-        for b in range(16):
-            first = 24 * b + 12 * cc
-            part[cc, b] = jnp.concatenate([left[first : first + 12], right[first : first + 12]], axis=0)
-
-    pl.semaphore_wait(barrier, 11)
+    for zb in range(4):
+        for xb in range(4):
+            for cc in (0, 1):
+                first = 24 * (4 * xb + zb) + 12 * cc
+                part[cc, zb, xb] = jnp.concatenate(
+                    [left[first : first + 12], right[first : first + 12]], axis=0
+                )
 
     sends = []
 
@@ -129,10 +141,10 @@
         sends.append(copy)
         return copy
 
-    order = (2, 1, 3, 0)
+    order = (0, 1, 3, 2)
     halves = []
     for i, d in enumerate(order):
-        block = pl.ds(((x + 2 + d) % 4) * 4, 4)
+        block = (z + d) % 4
         halves.append(send(i, part.at[other, block], part_in.at[i], partner, pair))
 
     loads[7].wait()
@@ -141,42 +153,58 @@
 
     arrivals = []
     for i, d in enumerate(order):
-        block = pl.ds(((x + 2 + d) % 4) * 4, 4)
+        block = (z + d) % 4
         halves[i].wait_recv()
         summed[block] = part[core, block] + part_in[i]
+        for dx in (2, 1, 3):
+            column = (x + 2 + dx) % 4
+            arrivals.append(
+                send(
+                    4 + 3 * i + dx - 1,
+                    summed.at[block, column],
+                    far_x_in.at[dx - 1, i],
+                    x_peers[dx - 1],
+                    pair,
+                )
+            )
+    pl.semaphore_wait(next_sem, 1)
+    for peer in z_peers:
+        signal(far_sem, peer, pair)
+    far = []
+    for i, d in enumerate(order):
+        if i == 1:
+            pl.semaphore_wait(far_sem, 3)
+        for copy in arrivals[3 * i : 3 * i + 3]:
+            copy.wait_recv()
+        kept = summed[(z + d) % 4, (x + 2) % 4]
+        far_x_sum[i] = kept + far_x_in[0, i] + far_x_in[1, i] + far_x_in[2, i]
+        far.append(send(16 + i, far_x_sum.at[i], far_in.at[i], far_peers[d], far_pair))
+
+    own_order = (2, 1, 3, 0)
+    arrivals = []
+    for i, d in enumerate(own_order):
+        for dx in (2, 1, 3):
+            column = (x + dx) % 4
+            arrivals.append(
+                send(
+                    20 + 3 * i + dx - 1,
+                    summed.at[(z + d) % 4, column],
+                    own_x_in.at[dx - 1, i],
+                    x_peers[dx - 1],
+                    pair,
+                )
+            )
+    own_z = []
+    for i, d in enumerate(own_order):
+        for copy in arrivals[3 * i : 3 * i + 3]:
+            copy.wait_recv()
+        kept = summed[(z + d) % 4, x] + own_x_in[0, i] + own_x_in[1, i] + own_x_in[2, i]
         if d:
-            arrivals.append(send(3 + d, summed.at[block], far_x_in.at[d - 1], x_peers[d - 1], pair))
-    for copy in arrivals:
+            own_x_sum[i] = kept
+            own_z.append(send(32 + i, own_x_sum.at[i], own_z_in.at[i], z_peers[d - 1], pair))
+    for copy in own_z:
         copy.wait_recv()
-    far_x_sum[...] = summed[pl.ds(((x + 2) % 4) * 4, 4)] + far_x_in[0] + far_x_in[1] + far_x_in[2]
-
-    far = []
-    for d in (0, 1, 3, 2):
-        copy = pltpu.make_async_remote_copy(
-            src_ref=far_x_sum.at[(z + d) % 4],
-            dst_ref=far_in.at[d],
-            send_sem=send_sem.at[7 + d],
-            recv_sem=recv_sem.at[7 + d],
-            device_id={"virt": far_peers[d], "pair": far_pair},
-            device_id_type=MESH,
-        )
-        copy.start()
-        sends.append(copy)
-        far.append(copy)
-
-    arrivals = []
-    for d in (2, 1, 3):
-        block = pl.ds(((x + d) % 4) * 4, 4)
-        arrivals.append(send(10 + d, summed.at[block], own_x_in.at[d - 1], x_peers[d - 1], pair))
-    for copy in arrivals:
-        copy.wait_recv()
-    own_x_sum[...] = summed[pl.ds(x * 4, 4)] + own_x_in[0] + own_x_in[1] + own_x_in[2]
-    arrivals = []
-    for d in (1, 2, 3):
-        arrivals.append(send(13 + d, own_x_sum.at[(z + d) % 4], own_z_in.at[d - 1], z_peers[d - 1], pair))
-    for copy in arrivals:
-        copy.wait_recv()
-    own = unpack(own_x_sum[z] + own_z_in[0] + own_z_in[1] + own_z_in[2])
+    own = unpack(kept + own_z_in[0] + own_z_in[1] + own_z_in[2])
 
     for copy in far:
         copy.wait_recv()
@@ -195,7 +223,7 @@
     any_spec = pl.BlockSpec(memory_space=pl.ANY)
     result = pl.pallas_call(
         kernel,
-        out_shape=jax.ShapeDtypeStruct((12, 256), F32),
+        out_shape=pltpu.VMEM((12, 256), F32),
         in_specs=[any_spec] * 4,
         out_specs=pl.BlockSpec(memory_space=pltpu.VMEM),
         scratch_shapes=[
@@ -203,19 +231,21 @@
             pltpu.VMEM((1920, 384), F32),
             pltpu.VMEM((4, 20), jnp.int32),
             pltpu.VMEM((1, 256), jnp.int32),
-            pltpu.VMEM((2, 16, 24, 128), F32),
+            pltpu.VMEM((2, 4, 4, 24, 128), F32),
             pltpu.VMEM((4, 4, 24, 128), F32),
-            pltpu.VMEM((16, 24, 128), F32),
+            pltpu.VMEM((4, 4, 24, 128), F32),
             pltpu.VMEM((3, 4, 24, 128), F32),
             pltpu.VMEM((4, 24, 128), F32),
             pltpu.VMEM((4, 24, 128), F32),
             pltpu.VMEM((3, 4, 24, 128), F32),
-            pltpu.VMEM((4, 24, 128), F32),
+            pltpu.VMEM((3, 24, 128), F32),
             pltpu.VMEM((3, 24, 128), F32),
             pltpu.VMEM((256, 256), BF16),
             pltpu.SemaphoreType.DMA((8,)),
-            pltpu.SemaphoreType.DMA((17,)),
-            pltpu.SemaphoreType.DMA((17,)),
+            pltpu.SemaphoreType.DMA((35,)),
+            pltpu.SemaphoreType.DMA((35,)),
+            pltpu.SemaphoreType.REGULAR,
+            pltpu.SemaphoreType.REGULAR,
         ],
         compiler_params=pltpu.CompilerParams(collective_id=0, has_side_effects=True),
         name="ladder",

time: 31.4 us -> 28.5 us (0.908)
  the two profiles are of different devices: /device:TPU:24 before, /device:TPU:1 now
where the time goes in v3:
time: 28.5 us; the launch traced here: 28.4 us
  Pallas kernels  27.8 us (98%)
  local copies, waits for them, and re-layouts  0.61 us (2%)
    pallas_call x1, Pallas kernels, shards(): pl.pallas_call(kernel, out_shape=pltpu.VMEM((12, 256), F32), in_specs=[an...  27.8 us
    unnamed x1, local copies, waits for them, and re-layouts  0.61 us

profile of v3, /device:TPU:1, one launch (start us, length us, event | category | flops | bytes accessed | tf_op | source)
XLA Modules:
  0.0 28.4 jit_solution(1237365555140916916)
XLA Ops:
  0.0 27.8 %ladder.1 = f32[12,256]{1,0:T(8,128)S(1)} custom-call(f32[256,1920]{1,0:T(8,128)} %amp_hbm.1, f32[1920,384]{1,0:T(8,128)} %int_hbm.1, s32[4,20]{1,0:T(4,128)} %bitcast.4, s32[1,256]{1,0:T(1,128)} %bitcast.5), custom_call_target="tpu_custom_call" | custom-call | tf_op jit(solution)/shard_map/ladder/pallas_call | solution.py:224
  27.8 0.6 %copy.6 = f32[256,12]{0,1:T(8,128)} copy(f32[256,12]{0,1:T(8,128)S(1)} %bitcast.3) | data formatting | bytes 24576

commit v4 on v3

--- a/solution.py
+++ b/solution.py
@@ -48,8 +48,7 @@
     load_sem,
     send_sem,
     recv_sem,
-    next_sem,
-    far_sem,
+    ready,
 ):
     loads = [pltpu.make_async_copy(mask_hbm, mask_in, load_sem.at[0])]
     for i, (start, size) in enumerate(CHUNKS):
@@ -81,18 +80,20 @@
     partner = at(x, z, other)
     x_peers = [at((x + d) % 4, z, core) for d in (1, 2, 3)]
     z_peers = [at(x, (z + d) % 4, core) for d in (1, 2, 3)]
-    far_peers = [at(x, (z + d) % 4, core) for d in (0, 1, 2, 3)]
-
+    far_peers = [at(x, d, core) for d in (0, 1, 2, 3)]
+
+    late = pair // 8
     barrier = pltpu.get_barrier_semaphore()
 
     def signal(semaphore, virt_to, pair_to):
         pl.semaphore_signal(semaphore, inc=1, device_id={"virt": virt_to, "pair": pair_to}, device_id_type=MESH)
 
-    next_pair = (pair + 4) % 16
-    last_pair = (pair + 12) % 16
-    signal(barrier, virt, next_pair)
-    signal(barrier, virt, last_pair)
-    for peer in [*z_peers, *x_peers, partner]:
+    @pl.when(late == 0)
+    def _():
+        for peer in far_peers:
+            signal(barrier, peer, far_pair)
+
+    for peer in [*x_peers, *z_peers, partner]:
         signal(barrier, peer, pair)
 
     lane_tile = lax.broadcasted_iota(jnp.int32, (4, 384), 1) // TILE
@@ -108,8 +109,13 @@
         loads[2 * i + 1].wait()
         loads[2 * i + 2].wait()
         if i == len(CHUNKS) - 1:
-            pl.semaphore_wait(barrier, 9)
-            signal(next_sem, virt, last_pair)
+            pl.semaphore_wait(barrier, 7 + 4 * late)
+
+            @pl.when(late == 1)
+            def _():
+                for peer in far_peers:
+                    signal(ready, peer, far_pair)
+
         tiles = []
         for t in range(start // TILE, (start + size) // TILE):
             tiles.append(ints[t * TILE : (t + 1) * TILE, :] * mask[t : t + 1, :])
@@ -141,10 +147,10 @@
         sends.append(copy)
         return copy
 
-    order = (0, 1, 3, 2)
+    order = (0, 1, 2, 3)
     halves = []
     for i, d in enumerate(order):
-        block = (z + d) % 4
+        block = d
         halves.append(send(i, part.at[other, block], part_in.at[i], partner, pair))
 
     loads[7].wait()
@@ -153,7 +159,7 @@
 
     arrivals = []
     for i, d in enumerate(order):
-        block = (z + d) % 4
+        block = d
         halves[i].wait_recv()
         summed[block] = part[core, block] + part_in[i]
         for dx in (2, 1, 3):
@@ -167,18 +173,27 @@
                     pair,
                 )
             )
-    pl.semaphore_wait(next_sem, 1)
-    for peer in z_peers:
-        signal(far_sem, peer, pair)
     far = []
     for i, d in enumerate(order):
-        if i == 1:
-            pl.semaphore_wait(far_sem, 3)
+        far.append(
+            pltpu.make_async_remote_copy(
+                src_ref=far_x_sum.at[i],
+                dst_ref=far_in.at[z],
+                send_sem=send_sem.at[16 + i],
+                recv_sem=recv_sem.at[16 + z],
+                device_id={"virt": far_peers[d], "pair": far_pair},
+                device_id_type=MESH,
+            )
+        )
+    for i, d in enumerate(order):
         for copy in arrivals[3 * i : 3 * i + 3]:
             copy.wait_recv()
-        kept = summed[(z + d) % 4, (x + 2) % 4]
+        kept = summed[d, (x + 2) % 4]
         far_x_sum[i] = kept + far_x_in[0, i] + far_x_in[1, i] + far_x_in[2, i]
-        far.append(send(16 + i, far_x_sum.at[i], far_in.at[i], far_peers[d], far_pair))
+
+        @pl.when(late == 1)
+        def _(copy=far[i]):
+            copy.start()
 
     own_order = (2, 1, 3, 0)
     arrivals = []
@@ -202,12 +217,18 @@
         if d:
             own_x_sum[i] = kept
             own_z.append(send(32 + i, own_x_sum.at[i], own_z_in.at[i], z_peers[d - 1], pair))
+    @pl.when(late == 0)
+    def _():
+        pl.semaphore_wait(ready, 4)
+        for copy in far:
+            copy.start()
+
     for copy in own_z:
         copy.wait_recv()
     own = unpack(kept + own_z_in[0] + own_z_in[1] + own_z_in[2])
 
-    for copy in far:
-        copy.wait_recv()
+    for slot in range(4):
+        pltpu.make_async_copy(far_in.at[slot], far_in.at[slot], recv_sem.at[16 + slot]).wait()
     turned = unpack(far_in[0] + far_in[1] + far_in[2] + far_in[3])
     first = turned.astype(BF16)
     rest = turned - first.astype(F32)
@@ -215,7 +236,7 @@
     matrix = select[...]
     out_ref[...] = own + (dot(first, matrix) + dot(second, matrix) + dot(third, matrix))
 
-    for copy in sends:
+    for copy in [*sends, *far]:
         copy.wait_send()
 
 
@@ -245,7 +266,6 @@
             pltpu.SemaphoreType.DMA((35,)),
             pltpu.SemaphoreType.DMA((35,)),
             pltpu.SemaphoreType.REGULAR,
-            pltpu.SemaphoreType.REGULAR,
         ],
         compiler_params=pltpu.CompilerParams(collective_id=0, has_side_effects=True),
         name="ladder",

time: 28.5 us -> 27.3 us (0.958)
  Pallas kernels: 27.8 us -> 26.6 us
    pallas_call x1, Pallas kernels: 27.8 us -> 26.6 us  [shards(): pl.pallas_call(kernel, out_shape=pltpu.VMEM((12, 256), F32), in_specs=[an...]
where the time goes in v4:
time: 27.3 us; the launch traced here: 27.2 us
  Pallas kernels  26.6 us (97%)
  local copies, waits for them, and re-layouts  0.61 us (2%)
    pallas_call x1, Pallas kernels, shards(): pl.pallas_call(kernel, out_shape=pltpu.VMEM((12, 256), F32), in_specs=[an...  26.6 us
    unnamed x1, local copies, waits for them, and re-layouts  0.61 us

profile of v4, /device:TPU:1, one launch (start us, length us, event | category | flops | bytes accessed | tf_op | source)
XLA Modules:
  0.0 27.2 jit_solution(8755503276074233359)
XLA Ops:
  0.0 26.6 %ladder.1 = f32[12,256]{1,0:T(8,128)S(1)} custom-call(f32[256,1920]{1,0:T(8,128)} %amp_hbm.1, f32[1920,384]{1,0:T(8,128)} %int_hbm.1, s32[4,20]{1,0:T(4,128)} %bitcast.4, s32[1,256]{1,0:T(1,128)} %bitcast.5), custom_call_target="tpu_custom_call" | custom-call | tf_op jit(solution)/shard_map/ladder/pallas_call | solution.py:245
  26.6 0.6 %copy.6 = f32[256,12]{0,1:T(8,128)} copy(f32[256,12]{0,1:T(8,128)S(1)} %bitcast.3) | data formatting | bytes 24576

commit v5 on v4

--- a/solution.py
+++ b/solution.py
@@ -39,6 +39,7 @@
     part_in,
     summed,
     far_x_in,
+    cross_in,
     far_x_sum,
     far_in,
     own_x_in,
@@ -79,6 +80,7 @@
 
     partner = at(x, z, other)
     x_peers = [at((x + d) % 4, z, core) for d in (1, 2, 3)]
+    cross_peers = [at((x + d) % 4, z, other) for d in (1, 2, 3)]
     z_peers = [at(x, (z + d) % 4, core) for d in (1, 2, 3)]
     far_peers = [at(x, d, core) for d in (0, 1, 2, 3)]
 
@@ -93,7 +95,7 @@
         for peer in far_peers:
             signal(barrier, peer, far_pair)
 
-    for peer in [*x_peers, *z_peers, partner]:
+    for peer in [*x_peers, *cross_peers, *z_peers, partner]:
         signal(barrier, peer, pair)
 
     lane_tile = lax.broadcasted_iota(jnp.int32, (4, 384), 1) // TILE
@@ -109,7 +111,7 @@
         loads[2 * i + 1].wait()
         loads[2 * i + 2].wait()
         if i == len(CHUNKS) - 1:
-            pl.semaphore_wait(barrier, 7 + 4 * late)
+            pl.semaphore_wait(barrier, 10 + 4 * late)
 
             @pl.when(late == 1)
             def _():
@@ -124,14 +126,6 @@
         total += dot(a_high, b_high) + dot(a_high, b_low) + dot(a_low, b_high)
     left = total[:128].T
     right = total[128:].T
-    for zb in range(4):
-        for xb in range(4):
-            for cc in (0, 1):
-                first = 24 * (4 * xb + zb) + 12 * cc
-                part[cc, zb, xb] = jnp.concatenate(
-                    [left[first : first + 12], right[first : first + 12]], axis=0
-                )
-
     sends = []
 
     def send(slot, src, dst, virt_to, pair_to):
@@ -147,32 +141,53 @@
         sends.append(copy)
         return copy
 
-    order = (0, 1, 2, 3)
-    halves = []
-    for i, d in enumerate(order):
-        block = d
-        halves.append(send(i, part.at[other, block], part_in.at[i], partner, pair))
+    halves = {}
+    arrivals = {zb: [] for zb in range(4)}
+
+    def pack(zb):
+        for xb in range(4):
+            for cc in (0, 1):
+                first = 24 * (4 * xb + zb) + 12 * cc
+                part[cc, zb, xb] = jnp.concatenate(
+                    [left[first : first + 12], right[first : first + 12]], axis=0
+                )
+
+    pack(0)
+    for dx in (2, 1, 3):
+        column = (x + 2 + dx) % 4
+        slot = dx - 1
+        arrivals[0].append(
+            send(4 + slot, part.at[core, 0, column], far_x_in.at[slot, 0], x_peers[slot], pair)
+        )
+        arrivals[0].append(
+            send(35 + slot, part.at[other, 0, column], cross_in.at[slot], cross_peers[slot], pair)
+        )
+    for zb in (1, 2, 3, 0):
+        if zb:
+            pack(zb)
+        halves[zb] = send(zb, part.at[other, zb], part_in.at[zb], partner, pair)
 
     loads[7].wait()
     rows = lax.broadcasted_iota(jnp.int32, (256, 256), 0)
     select[...] = (rows == mirror_row[...]).astype(F32).astype(BF16)
 
-    arrivals = []
-    for i, d in enumerate(order):
-        block = d
-        halves[i].wait_recv()
-        summed[block] = part[core, block] + part_in[i]
-        for dx in (2, 1, 3):
-            column = (x + 2 + dx) % 4
-            arrivals.append(
-                send(
-                    4 + 3 * i + dx - 1,
-                    summed.at[block, column],
-                    far_x_in.at[dx - 1, i],
-                    x_peers[dx - 1],
-                    pair,
+    for zb in (1, 2, 3, 0):
+        halves[zb].wait_recv()
+        summed[zb] = part[core, zb] + part_in[zb]
+        if zb:
+            for dx in (2, 1, 3):
+                column = (x + 2 + dx) % 4
+                slot = dx - 1
+                arrivals[zb].append(
+                    send(
+                        4 + 3 * zb + slot,
+                        summed.at[zb, column],
+                        far_x_in.at[slot, zb],
+                        x_peers[slot],
+                        pair,
+                    )
                 )
-            )
+    order = (0, 1, 2, 3)
     far = []
     for i, d in enumerate(order):
         far.append(
@@ -186,10 +201,12 @@
             )
         )
     for i, d in enumerate(order):
-        for copy in arrivals[3 * i : 3 * i + 3]:
+        for copy in arrivals[d]:
             copy.wait_recv()
-        kept = summed[d, (x + 2) % 4]
-        far_x_sum[i] = kept + far_x_in[0, i] + far_x_in[1, i] + far_x_in[2, i]
+        kept = summed[d, (x + 2) % 4] + far_x_in[0, i] + far_x_in[1, i] + far_x_in[2, i]
+        if d == 0:
+            kept += cross_in[0] + cross_in[1] + cross_in[2]
+        far_x_sum[i] = kept
 
         @pl.when(late == 1)
         def _(copy=far[i]):
@@ -227,17 +244,17 @@
         copy.wait_recv()
     own = unpack(kept + own_z_in[0] + own_z_in[1] + own_z_in[2])
 
+    for copy in [*sends, *far]:
+        copy.wait_send()
+
     for slot in range(4):
         pltpu.make_async_copy(far_in.at[slot], far_in.at[slot], recv_sem.at[16 + slot]).wait()
     turned = unpack(far_in[0] + far_in[1] + far_in[2] + far_in[3])
+    turned = jnp.concatenate([turned, jnp.zeros((4, 256), F32)], axis=0)
     first = turned.astype(BF16)
-    rest = turned - first.astype(F32)
-    second, third = split(rest)
-    matrix = select[...]
-    out_ref[...] = own + (dot(first, matrix) + dot(second, matrix) + dot(third, matrix))
-
-    for copy in [*sends, *far]:
-        copy.wait_send()
+    second, third = split(turned - first.astype(F32))
+    moved = dot(jnp.concatenate([first, second, third], axis=0), select[...])
+    out_ref[...] = own + (moved[0:12] + moved[16:28] + moved[32:44])
 
 
 def shards(amplitudes, integrals, tile_mask, mirror_row):
@@ -256,6 +273,7 @@
             pltpu.VMEM((4, 4, 24, 128), F32),
             pltpu.VMEM((4, 4, 24, 128), F32),
             pltpu.VMEM((3, 4, 24, 128), F32),
+            pltpu.VMEM((3, 24, 128), F32),
             pltpu.VMEM((4, 24, 128), F32),
             pltpu.VMEM((4, 24, 128), F32),
             pltpu.VMEM((3, 4, 24, 128), F32),
@@ -263,8 +281,8 @@
             pltpu.VMEM((3, 24, 128), F32),
             pltpu.VMEM((256, 256), BF16),
             pltpu.SemaphoreType.DMA((8,)),
-            pltpu.SemaphoreType.DMA((35,)),
-            pltpu.SemaphoreType.DMA((35,)),
+            pltpu.SemaphoreType.DMA((38,)),
+            pltpu.SemaphoreType.DMA((38,)),
             pltpu.SemaphoreType.REGULAR,
         ],
         compiler_params=pltpu.CompilerParams(collective_id=0, has_side_effects=True),

time: 27.3 us -> 26.5 us (0.971)
  Pallas kernels: 26.6 us -> 25.8 us
    pallas_call x1, Pallas kernels: 26.6 us -> 25.8 us  [shards(): pl.pallas_call(kernel, out_shape=pltpu.VMEM((12, 256), F32), in_specs=[an...]
where the time goes in v5:
time: 26.5 us; the launch traced here: 26.4 us
  Pallas kernels  25.8 us (97%)
  local copies, waits for them, and re-layouts  0.61 us (2%)
    pallas_call x1, Pallas kernels, shards(): pl.pallas_call(kernel, out_shape=pltpu.VMEM((12, 256), F32), in_specs=[an...  25.8 us
    unnamed x1, local copies, waits for them, and re-layouts  0.61 us

profile of v5, /device:TPU:1, one launch (start us, length us, event | category | flops | bytes accessed | tf_op | source)
XLA Modules:
  0.0 26.4 jit_solution(6181976283033566556)
XLA Ops:
  0.0 25.8 %ladder.1 = f32[12,256]{1,0:T(8,128)S(1)} custom-call(f32[256,1920]{1,0:T(8,128)} %amp_hbm.1, f32[1920,384]{1,0:T(8,128)} %int_hbm.1, s32[4,20]{1,0:T(4,128)} %bitcast.4, s32[1,256]{1,0:T(1,128)} %bitcast.5), custom_call_target="tpu_custom_call" | custom-call | tf_op jit(solution)/shard_map/ladder/pallas_call | solution.py:262
  25.8 0.6 %copy.6 = f32[256,12]{0,1:T(8,128)} copy(f32[256,12]{0,1:T(8,128)S(1)} %bitcast.3) | data formatting | bytes 24576

commit v6 on v5

--- a/solution.py
+++ b/solution.py
@@ -6,7 +6,7 @@
 from jax.sharding import PartitionSpec as P
 
 TILE = 96
-CHUNKS = ((0, 768), (768, 768), (1536, 384))
+CHUNKS = ((0, 256), (256, 512), (768, 768), (1536, 384))
 F32 = jnp.float32
 BF16 = jnp.bfloat16
 MESH = pl.DeviceIdType.MESH
@@ -63,9 +63,9 @@
                 amp_hbm.at[:, pl.ds(start, size)], amp.at[:, pl.ds(start, size)], load_sem.at[2 * i + 2]
             )
         )
-    loads.append(pltpu.make_async_copy(mirror_hbm, mirror_row, load_sem.at[7]))
-    for load in loads:
-        load.start()
+    loads.append(pltpu.make_async_copy(mirror_hbm, mirror_row, load_sem.at[9]))
+    for i, load in enumerate(loads):
+        load.start(priority=int(i > 2))
 
     virt = lax.axis_index("virt")
     pair = lax.axis_index("pair")
@@ -119,11 +119,14 @@
                     signal(ready, peer, far_pair)
 
         tiles = []
-        for t in range(start // TILE, (start + size) // TILE):
-            tiles.append(ints[t * TILE : (t + 1) * TILE, :] * mask[t : t + 1, :])
+        edges = sorted({start, start + size, *range(-(-start // TILE) * TILE, start + size, TILE)})
+        for low, high in zip(edges, edges[1:]):
+            t = low // TILE
+            tiles.append(ints[low:high, :] * mask[t : t + 1, :])
         b_high, b_low = split(jnp.concatenate(tiles, axis=0))
         a_high, a_low = split(amp[:, start : start + size])
-        total += dot(a_high, b_high) + dot(a_high, b_low) + dot(a_low, b_high)
+        both = dot(a_high, jnp.concatenate([b_high, b_low], axis=1))
+        total += both[:, :384] + both[:, 384:] + dot(a_low, b_high)
     left = total[:128].T
     right = total[128:].T
     sends = []
@@ -167,7 +170,7 @@
             pack(zb)
         halves[zb] = send(zb, part.at[other, zb], part_in.at[zb], partner, pair)
 
-    loads[7].wait()
+    loads[9].wait()
     rows = lax.broadcasted_iota(jnp.int32, (256, 256), 0)
     select[...] = (rows == mirror_row[...]).astype(F32).astype(BF16)
 
@@ -280,7 +283,7 @@
             pltpu.VMEM((3, 24, 128), F32),
             pltpu.VMEM((3, 24, 128), F32),
             pltpu.VMEM((256, 256), BF16),
-            pltpu.SemaphoreType.DMA((8,)),
+            pltpu.SemaphoreType.DMA((10,)),
             pltpu.SemaphoreType.DMA((38,)),
             pltpu.SemaphoreType.DMA((38,)),
             pltpu.SemaphoreType.REGULAR,

time: 26.5 us -> 26.2 us (0.989)
  Pallas kernels: 25.8 us -> 25.5 us
    pallas_call x1, Pallas kernels: 25.8 us -> 25.5 us  [shards(): pl.pallas_call(kernel, out_shape=pltpu.VMEM((12, 256), F32), in_specs=[an...]
where the time goes in v6:
time: 26.2 us; the launch traced here: 26.1 us
  Pallas kernels  25.5 us (97%)
  local copies, waits for them, and re-layouts  0.61 us (2%)
    pallas_call x1, Pallas kernels, shards(): pl.pallas_call(kernel, out_shape=pltpu.VMEM((12, 256), F32), in_specs=[an...  25.5 us
    unnamed x1, local copies, waits for them, and re-layouts  0.61 us

profile of v6, /device:TPU:1, one launch (start us, length us, event | category | flops | bytes accessed | tf_op | source)
XLA Modules:
  0.0 26.1 jit_solution(5606594049865839264)
XLA Ops:
  0.0 25.5 %ladder.1 = f32[12,256]{1,0:T(8,128)S(1)} custom-call(f32[256,1920]{1,0:T(8,128)} %amp_hbm.1, f32[1920,384]{1,0:T(8,128)} %int_hbm.1, s32[4,20]{1,0:T(4,128)} %bitcast.4, s32[1,256]{1,0:T(1,128)} %bitcast.5), custom_call_target="tpu_custom_call" | custom-call | tf_op jit(solution)/shard_map/ladder/pallas_call | solution.py:265
  25.5 0.6 %copy.6 = f32[256,12]{0,1:T(8,128)} copy(f32[256,12]{0,1:T(8,128)S(1)} %bitcast.3) | data formatting | bytes 24576

commit v7 on v6

--- a/solution.py
+++ b/solution.py
@@ -40,6 +40,8 @@
     summed,
     far_x_in,
     cross_in,
+    straight_in,
+    arrived,
     far_x_sum,
     far_in,
     own_x_in,
@@ -85,6 +87,9 @@
     far_peers = [at(x, d, core) for d in (0, 1, 2, 3)]
 
     late = pair // 8
+    even = 1 - (pair // 4) % 2
+    straight = [even * (z == zb).astype(jnp.int32) for zb in range(4)]
+    straight_peer = at((x + 2) % 4, z, core)
     barrier = pltpu.get_barrier_semaphore()
 
     def signal(semaphore, virt_to, pair_to):
@@ -94,6 +99,10 @@
     def _():
         for peer in far_peers:
             signal(barrier, peer, far_pair)
+
+        @pl.when(even == 1)
+        def _():
+            signal(barrier, straight_peer, far_pair)
 
     for peer in [*x_peers, *cross_peers, *z_peers, partner]:
         signal(barrier, peer, pair)
@@ -111,12 +120,16 @@
         loads[2 * i + 1].wait()
         loads[2 * i + 2].wait()
         if i == len(CHUNKS) - 1:
-            pl.semaphore_wait(barrier, 10 + 4 * late)
+            pl.semaphore_wait(barrier, 10 + (4 + even) * late)
 
             @pl.when(late == 1)
             def _():
                 for peer in far_peers:
                     signal(ready, peer, far_pair)
+
+                @pl.when(even == 1)
+                def _():
+                    signal(ready, straight_peer, far_pair)
 
         tiles = []
         edges = sorted({start, start + size, *range(-(-start // TILE) * TILE, start + size, TILE)})
@@ -131,8 +144,8 @@
     right = total[128:].T
     sends = []
 
-    def send(slot, src, dst, virt_to, pair_to):
-        copy = pltpu.make_async_remote_copy(
+    def describe(slot, src, dst, virt_to, pair_to):
+        return pltpu.make_async_remote_copy(
             src_ref=src,
             dst_ref=dst,
             send_sem=send_sem.at[slot],
@@ -140,6 +153,9 @@
             device_id={"virt": virt_to, "pair": pair_to},
             device_id_type=MESH,
         )
+
+    def send(*where):
+        copy = describe(*where)
         copy.start()
         sends.append(copy)
         return copy
@@ -155,17 +171,38 @@
                     [left[first : first + 12], right[first : first + 12]], axis=0
                 )
 
-    pack(0)
-    for dx in (2, 1, 3):
+    def across(zb, dx, use_part):
         column = (x + 2 + dx) % 4
         slot = dx - 1
-        arrivals[0].append(
-            send(4 + slot, part.at[core, 0, column], far_x_in.at[slot, 0], x_peers[slot], pair)
-        )
-        arrivals[0].append(
-            send(35 + slot, part.at[other, 0, column], cross_in.at[slot], cross_peers[slot], pair)
-        )
-    for zb in (1, 2, 3, 0):
+        src = part.at[core, zb, column] if use_part else summed.at[zb, column]
+        copies = [describe(4 + 3 * zb + slot, src, far_x_in.at[slot, zb], x_peers[slot], pair)]
+        if use_part:
+            copies.append(
+                describe(35 + slot, part.at[other, zb, column], cross_in.at[slot], cross_peers[slot], pair)
+            )
+        return copies
+
+    long_x = {zb: across(zb, 2, zb == 0) for zb in range(4)}
+
+    def start_long(zb):
+        @pl.when(straight[zb] == 0)
+        def _():
+            for copy in long_x[zb]:
+                copy.start()
+
+    def start_short(zb):
+        for dx in (1, 3):
+            for copy in across(zb, dx, zb == 0):
+                copy.start()
+                sends.append(copy)
+                arrivals[zb].append(copy)
+
+    direct = describe(38, summed.at[z, x], straight_in, straight_peer, far_pair)
+
+    pack(0)
+    start_long(0)
+    start_short(0)
+    for zb in range(4):
         if zb:
             pack(zb)
         halves[zb] = send(zb, part.at[other, zb], part_in.at[zb], partner, pair)
@@ -174,22 +211,18 @@
     rows = lax.broadcasted_iota(jnp.int32, (256, 256), 0)
     select[...] = (rows == mirror_row[...]).astype(F32).astype(BF16)
 
-    for zb in (1, 2, 3, 0):
+    for zb in (0, 1, 2, 3):
         halves[zb].wait_recv()
         summed[zb] = part[core, zb] + part_in[zb]
+
+        @pl.when(straight[zb] * late == 1)
+        def _():
+            direct.start()
+
         if zb:
-            for dx in (2, 1, 3):
-                column = (x + 2 + dx) % 4
-                slot = dx - 1
-                arrivals[zb].append(
-                    send(
-                        4 + 3 * zb + slot,
-                        summed.at[zb, column],
-                        far_x_in.at[slot, zb],
-                        x_peers[slot],
-                        pair,
-                    )
-                )
+            start_long(zb)
+            start_short(zb)
+
     order = (0, 1, 2, 3)
     far = []
     for i, d in enumerate(order):
@@ -206,10 +239,19 @@
     for i, d in enumerate(order):
         for copy in arrivals[d]:
             copy.wait_recv()
-        kept = summed[d, (x + 2) % 4] + far_x_in[0, i] + far_x_in[1, i] + far_x_in[2, i]
+        kept = summed[d, (x + 2) % 4] + far_x_in[0, i] + far_x_in[2, i]
         if d == 0:
-            kept += cross_in[0] + cross_in[1] + cross_in[2]
+            kept += cross_in[0] + cross_in[2]
         far_x_sum[i] = kept
+
+        @pl.when(straight[d] == 0)
+        def _():
+            for copy in long_x[d]:
+                copy.wait_recv()
+            more = far_x_in[1, d]
+            if d == 0:
+                more += cross_in[1]
+            far_x_sum[d] += more
 
         @pl.when(late == 1)
         def _(copy=far[i]):
@@ -239,9 +281,13 @@
             own_z.append(send(32 + i, own_x_sum.at[i], own_z_in.at[i], z_peers[d - 1], pair))
     @pl.when(late == 0)
     def _():
-        pl.semaphore_wait(ready, 4)
+        pl.semaphore_wait(ready, 4 + even)
         for copy in far:
             copy.start()
+
+        @pl.when(even == 1)
+        def _():
+            direct.start()
 
     for copy in own_z:
         copy.wait_recv()
@@ -249,10 +295,23 @@
 
     for copy in [*sends, *far]:
         copy.wait_send()
+    for zb in range(4):
+        @pl.when(straight[zb] == 0)
+        def _():
+            for copy in long_x[zb]:
+                copy.wait_send()
+
 
     for slot in range(4):
         pltpu.make_async_copy(far_in.at[slot], far_in.at[slot], recv_sem.at[16 + slot]).wait()
-    turned = unpack(far_in[0] + far_in[1] + far_in[2] + far_in[3])
+    arrived[...] = far_in[0] + far_in[1] + far_in[2] + far_in[3]
+
+    @pl.when(even == 1)
+    def _():
+        direct.wait()
+        arrived[...] += straight_in[...]
+
+    turned = unpack(arrived[...])
     turned = jnp.concatenate([turned, jnp.zeros((4, 256), F32)], axis=0)
     first = turned.astype(BF16)
     second, third = split(turned - first.astype(F32))
@@ -277,6 +336,8 @@
             pltpu.VMEM((4, 4, 24, 128), F32),
             pltpu.VMEM((3, 4, 24, 128), F32),
             pltpu.VMEM((3, 24, 128), F32),
+            pltpu.VMEM((24, 128), F32),
+            pltpu.VMEM((24, 128), F32),
             pltpu.VMEM((4, 24, 128), F32),
             pltpu.VMEM((4, 24, 128), F32),
             pltpu.VMEM((3, 4, 24, 128), F32),
@@ -284,8 +345,8 @@
             pltpu.VMEM((3, 24, 128), F32),
             pltpu.VMEM((256, 256), BF16),
             pltpu.SemaphoreType.DMA((10,)),
-            pltpu.SemaphoreType.DMA((38,)),
-            pltpu.SemaphoreType.DMA((38,)),
+            pltpu.SemaphoreType.DMA((39,)),
+            pltpu.SemaphoreType.DMA((39,)),
             pltpu.SemaphoreType.REGULAR,
         ],
         compiler_params=pltpu.CompilerParams(collective_id=0, has_side_effects=True),

time: 26.2 us -> 26.1 us (level)
  no operation moved by 1% of the time
where the time goes in v7:
time: 26.1 us; the launch traced here: 26 us
  Pallas kernels  25.3 us (97%)
  local copies, waits for them, and re-layouts  0.61 us (2%)
    pallas_call x1, Pallas kernels, shards(): pl.pallas_call(kernel, out_shape=pltpu.VMEM((12, 256), F32), in_specs=[an...  25.3 us
    unnamed x1, local copies, waits for them, and re-layouts  0.61 us

profile of v7, /device:TPU:1, one launch (start us, length us, event | category | flops | bytes accessed | tf_op | source)
XLA Modules:
  0.0 26.0 jit_solution(6552956956106318896)
XLA Ops:
  0.0 25.3 %ladder.1 = f32[12,256]{1,0:T(8,128)S(1)} custom-call(f32[256,1920]{1,0:T(8,128)} %amp_hbm.1, f32[1920,384]{1,0:T(8,128)} %int_hbm.1, s32[4,20]{1,0:T(4,128)} %bitcast.4, s32[1,256]{1,0:T(1,128)} %bitcast.5), custom_call_target="tpu_custom_call" | custom-call | tf_op jit(solution)/shard_map/ladder/pallas_call | solution.py:324
  25.4 0.6 %copy.6 = f32[256,12]{0,1:T(8,128)} copy(f32[256,12]{0,1:T(8,128)S(1)} %bitcast.3) | data formatting | bytes 24576

commit v8 on v7

--- a/solution.py
+++ b/solution.py
@@ -122,15 +122,6 @@
         if i == len(CHUNKS) - 1:
             pl.semaphore_wait(barrier, 10 + (4 + even) * late)
 
-            @pl.when(late == 1)
-            def _():
-                for peer in far_peers:
-                    signal(ready, peer, far_pair)
-
-                @pl.when(even == 1)
-                def _():
-                    signal(ready, straight_peer, far_pair)
-
         tiles = []
         edges = sorted({start, start + size, *range(-(-start // TILE) * TILE, start + size, TILE)})
         for low, high in zip(edges, edges[1:]):
@@ -138,10 +129,15 @@
             tiles.append(ints[low:high, :] * mask[t : t + 1, :])
         b_high, b_low = split(jnp.concatenate(tiles, axis=0))
         a_high, a_low = split(amp[:, start : start + size])
-        both = dot(a_high, jnp.concatenate([b_high, b_low], axis=1))
-        total += both[:, :384] + both[:, 384:] + dot(a_low, b_high)
-    left = total[:128].T
-    right = total[128:].T
+        b_both = jnp.concatenate([b_high, b_low], axis=1)
+        if i < len(CHUNKS) - 1:
+            both = dot(a_high, b_both)
+            total += both[:, :384] + both[:, 384:] + dot(a_low, b_high)
+    sides = []
+    for rows in (slice(0, 128), slice(128, 256)):
+        both = dot(a_high[rows], b_both)
+        sides.append((total[rows] + both[:, :384] + both[:, 384:] + dot(a_low[rows], b_high)).T)
+    left, right = sides
     sends = []
 
     def describe(slot, src, dst, virt_to, pair_to):
@@ -202,16 +198,25 @@
     pack(0)
     start_long(0)
     start_short(0)
-    for zb in range(4):
+    for zb in (1, 0, 2, 3):
         if zb:
             pack(zb)
         halves[zb] = send(zb, part.at[other, zb], part_in.at[zb], partner, pair)
 
+    @pl.when(late == 1)
+    def _():
+        for peer in far_peers:
+            signal(ready, peer, far_pair)
+
+        @pl.when(even == 1)
+        def _():
+            signal(ready, straight_peer, far_pair)
+
     loads[9].wait()
     rows = lax.broadcasted_iota(jnp.int32, (256, 256), 0)
     select[...] = (rows == mirror_row[...]).astype(F32).astype(BF16)
 
-    for zb in (0, 1, 2, 3):
+    for zb in (1, 0, 2, 3):
         halves[zb].wait_recv()
         summed[zb] = part[core, zb] + part_in[zb]
 

time: 26.1 us -> 26.1 us (level)
  no operation moved by 1% of the time
where the time goes in v8:
time: 26.1 us; the launch traced here: 26 us
  Pallas kernels  25.4 us (97%)
  local copies, waits for them, and re-layouts  0.61 us (2%)
    pallas_call x1, Pallas kernels, shards(): pl.pallas_call(kernel, out_shape=pltpu.VMEM((12, 256), F32), in_specs=[an...  25.4 us
    unnamed x1, local copies, waits for them, and re-layouts  0.61 us

profile of v8, /device:TPU:1, one launch (start us, length us, event | category | flops | bytes accessed | tf_op | source)
XLA Modules:
  0.0 26.0 jit_solution(12486594843706250576)
XLA Ops:
  0.0 25.4 %ladder.1 = f32[12,256]{1,0:T(8,128)S(1)} custom-call(f32[256,1920]{1,0:T(8,128)} %amp_hbm.1, f32[1920,384]{1,0:T(8,128)} %int_hbm.1, s32[4,20]{1,0:T(4,128)} %bitcast.4, s32[1,256]{1,0:T(1,128)} %bitcast.5), custom_call_target="tpu_custom_call" | custom-call | tf_op jit(solution)/shard_map/ladder/pallas_call | solution.py:329
  25.4 0.6 %copy.6 = f32[256,12]{0,1:T(8,128)} copy(f32[256,12]{0,1:T(8,128)S(1)} %bitcast.3) | data formatting | bytes 24576

commit v9 on v7

--- a/solution.py
+++ b/solution.py
@@ -202,7 +202,7 @@
     pack(0)
     start_long(0)
     start_short(0)
-    for zb in range(4):
+    for zb in (1, 0, 2, 3):
         if zb:
             pack(zb)
         halves[zb] = send(zb, part.at[other, zb], part_in.at[zb], partner, pair)
@@ -211,7 +211,7 @@
     rows = lax.broadcasted_iota(jnp.int32, (256, 256), 0)
     select[...] = (rows == mirror_row[...]).astype(F32).astype(BF16)
 
-    for zb in (0, 1, 2, 3):
+    for zb in (1, 0, 2, 3):
         halves[zb].wait_recv()
         summed[zb] = part[core, zb] + part_in[zb]
 

time: 26.1 us -> 26 us (level)
  no operation moved by 1% of the time
where the time goes in v9:
time: 26 us; the launch traced here: 25.9 us
  Pallas kernels  25.3 us (97%)
  local copies, waits for them, and re-layouts  0.61 us (2%)
    pallas_call x1, Pallas kernels, shards(): pl.pallas_call(kernel, out_shape=pltpu.VMEM((12, 256), F32), in_specs=[an...  25.3 us
    unnamed x1, local copies, waits for them, and re-layouts  0.61 us

profile of v9, /device:TPU:1, one launch (start us, length us, event | category | flops | bytes accessed | tf_op | source)
XLA Modules:
  0.0 25.9 jit_solution(731033500144112021)
XLA Ops:
  0.0 25.3 %ladder.1 = f32[12,256]{1,0:T(8,128)S(1)} custom-call(f32[256,1920]{1,0:T(8,128)} %amp_hbm.1, f32[1920,384]{1,0:T(8,128)} %int_hbm.1, s32[4,20]{1,0:T(4,128)} %bitcast.4, s32[1,256]{1,0:T(1,128)} %bitcast.5), custom_call_target="tpu_custom_call" | custom-call | tf_op jit(solution)/shard_map/ladder/pallas_call | solution.py:324
  25.3 0.6 %copy.6 = f32[256,12]{0,1:T(8,128)} copy(f32[256,12]{0,1:T(8,128)S(1)} %bitcast.3) | data formatting | bytes 24576
